TPU v7x, 256 devices: a whole 4x4x8 slice. The times are simulated.
256 devices in a mesh: layer: 16 (over z_hi, y, core), phi: 16 (over x, z_lo).
Axes of the slice: x: 4, y: 4, z: 8 (z_hi: 2, z_lo: 4; z = z_hi * 4 + z_lo), core: 2. Of those that a mesh axis runs over, the one named last changes fastest.
Arguments:
- features: bfloat16 [65536, 256], P(('layer', 'phi')), may hold values from -6 to 6
- w_layers: bfloat16 [4, 256, 256], replicated, may hold values from -0.375 to 0.375
- b_layers: float32 [4, 256], replicated, may hold values from -1.5 to 1.5
- w_coord: bfloat16 [16, 256], replicated, may hold values from -0.09375 to 0.09375
- w_beta: bfloat16 [256], replicated, may hold values from -0.375 to 0.375
- point_hit: int32 [2048], P(('layer', 'phi')), may hold values from 0 to 255
- track: int32 [65536], P(('layer', 'phi')), may hold values from 0 to 2047
- noise: int32 [65536], P(('layer', 'phi')), may hold values 0 or 1
Outputs:
- grad_w_layers: float32 [4, 256, 256], replicated
- grad_b_layers: float32 [4, 256], replicated
- grad_w_coord: float32 [16, 256], replicated
- grad_w_beta: float32 [256], replicated
- loss: float32 [], replicated
Inputs may be any that keep to these rules, and one draw needn't show every extreme that they name: `point_hit`: an index among the 256 hits of the device holding the entry. A non-noise hit of track k is attracted to point k.
All inputs are finite; a program needn't handle non-finite values. No bound on the sum of `noise` on one device may be relied on, other than what follows from the above.
Results may differ from a plain program's by a relative error of at most 0.0013.
Values sent between devices are 32-bit elements; how exact they have to be, the bound alone decides.
A program may use at most 64 MiB of HBM per device.

v0:
```python
import jax
import jax.numpy as jnp
from jax import lax
from jax.sharding import PartitionSpec as P

dist_eps = 0.0001
charge_floor = 0.5
block_cols = 512


def mlp_forward(features, w_layers, b_layers, w_coord, w_beta):
    hidden = features
    states = [features]
    preacts = []
    for layer_num in range(w_layers.shape[0]):
        pre = (
            jnp.dot(hidden, w_layers[layer_num], preferred_element_type=jnp.float32)
            + b_layers[layer_num]
        )
        preacts.append(pre)
        hidden = jax.nn.silu(pre).astype(jnp.bfloat16)
        states.append(hidden)
    coords = lax.dot_general(
        w_coord, hidden, (((1,), (1,)), ((), ())), preferred_element_type=jnp.float32
    )
    logits = jnp.dot(hidden, w_beta, preferred_element_type=jnp.float32)
    return (states, preacts, coords, logits)


def charges(logits):
    expz = jnp.exp(logits)
    spread = jnp.log1p(2.0 * expz)
    charge = 0.25 * spread * spread + charge_floor
    slope = 0.5 * spread * (2.0 * expz / (1.0 + 2.0 * expz))
    return (jax.nn.sigmoid(logits), charge, slope)


def pair_terms(coords, charge, track, live, point_rows, first, hits_all):
    point_y = point_rows[:-1]
    point_q = point_rows[-1]
    width = point_rows.shape[1]
    hit_sq = jnp.sum(coords * coords, 0)
    point_sq = jnp.sum(point_y * point_y, 0)
    cross = lax.dot_general(
        coords,
        point_y,
        (((0,), (0,)), ((), ())),
        precision=lax.Precision.HIGHEST,
        preferred_element_type=jnp.float32,
    )
    dist_sq = jnp.maximum(hit_sq[:, None] + point_sq[None, :] - 2.0 * cross, 0.0)
    dist = jnp.sqrt(dist_sq + dist_eps)
    index = first + lax.iota(jnp.int32, width)
    match = jnp.where((track[:, None] == index[None, :]) & (live[:, None] > 0), 1.0, 0.0)
    reach = jnp.maximum(1.0 - dist, 0.0)
    potential = match * dist_sq + (1.0 - match) * reach * reach
    pot_rows = jnp.sum(potential * point_q[None, :], 1)
    coef = (
        (charge / hits_all)[:, None]
        * point_q[None, :]
        * (2.0 * match - (1.0 - match) * 2.0 * reach / dist)
    )
    row_sums = jnp.sum(coef, 1)
    col_sums = jnp.sum(coef, 0)
    pulls = lax.dot_general(
        point_y,
        coef,
        (((1,), (1,)), ((), ())),
        precision=lax.Precision.HIGHEST,
        preferred_element_type=jnp.float32,
    )
    point_grad = point_y * col_sums[None, :] - lax.dot_general(
        coords,
        coef,
        (((1,), (0,)), ((), ())),
        precision=lax.Precision.HIGHEST,
        preferred_element_type=jnp.float32,
    )
    charge_grad = jnp.dot(charge, potential, precision=lax.Precision.HIGHEST) / hits_all
    return (row_sums, pot_rows, pulls, jnp.concatenate([point_grad, charge_grad[None, :]], 0))


def on_device(features, w_layers, b_layers, w_coord, w_beta, point_hit, track, noise):
    hit_count = features.shape[0]
    point_count = point_hit.shape[0]
    ndev = lax.axis_size("layer") * lax.axis_size("phi")
    total_points = point_count * ndev
    hits_all = hit_count * ndev * 1.0
    states, preacts, coords, logits = mlp_forward(features, w_layers, b_layers, w_coord, w_beta)
    beta_vals, charge, slope = charges(logits)
    selector = jnp.where(point_hit[:, None] == lax.iota(jnp.int32, hit_count)[None, :], 1.0, 0.0)
    own_y = lax.dot_general(
        coords,
        selector,
        (((1,), (1,)), ((), ())),
        precision=lax.Precision.HIGHEST,
        preferred_element_type=jnp.float32,
    )
    own_q = jnp.dot(selector, charge, precision=lax.Precision.HIGHEST)
    own_beta = jnp.dot(selector, beta_vals, precision=lax.Precision.HIGHEST)
    own_rows = jnp.concatenate([own_y, own_q[None, :]], 0)
    live = 1 - noise
    init = (
        jnp.zeros((hit_count,), jnp.float32),
        jnp.zeros((hit_count,), jnp.float32),
        jnp.zeros(coords.shape, jnp.float32),
        jnp.zeros((own_rows.shape[0], total_points), jnp.float32),
    )
    piece = lax.all_gather(own_rows, ("layer", "phi"), axis=1, tiled=True)
    width = piece.shape[1]

    def one_block(state, offset, cols):
        row_acc, pot_acc, pull_acc, grad_acc = state
        block = lax.dynamic_slice_in_dim(piece, offset, cols, 1)
        row_sums, pot_rows, pulls, point_grads = pair_terms(
            coords, charge, track, live, block, offset, hits_all
        )
        grad_acc = lax.dynamic_update_slice_in_dim(grad_acc, point_grads, offset, 1)
        return (row_acc + row_sums, pot_acc + pot_rows, pull_acc + pulls, grad_acc)

    full = width // block_cols
    state = init
    state = lax.fori_loop(
        0, full, lambda step, inner: one_block(inner, step * block_cols, block_cols), state
    )
    row_sums, pot_rows, pulls, point_grads = state
    own_grads = lax.psum_scatter(point_grads, ("layer", "phi"), scatter_dimension=1, tiled=True)
    coord_dim = coords.shape[0]
    coord_grad = coords * row_sums[None, :] - pulls
    coord_grad = coord_grad + jnp.dot(
        own_grads[:coord_dim], selector, precision=lax.Precision.HIGHEST
    )
    charge_grad = pot_rows / hits_all + jnp.dot(
        own_grads[coord_dim], selector, precision=lax.Precision.HIGHEST
    )
    noise_float = noise.astype(jnp.float32)
    beta_grad = noise_float / hits_all + jnp.sum(selector, 0) * (-1.0 / total_points)
    logit_grad = charge_grad * slope + beta_grad * beta_vals * (1.0 - beta_vals)
    loss_local = (
        jnp.sum(charge * pot_rows) / hits_all
        + jnp.sum(1.0 - own_beta) / total_points
        + jnp.sum(noise_float * beta_vals) / hits_all
    )
    coord_low = coord_grad.astype(jnp.bfloat16)
    logit_low = logit_grad.astype(jnp.bfloat16)
    hidden = states[-1]
    grad_coord_w = lax.dot_general(
        coord_low, hidden, (((1,), (0,)), ((), ())), preferred_element_type=jnp.float32
    )
    grad_beta_w = jnp.dot(logit_low, hidden, preferred_element_type=jnp.float32)
    upstream = lax.dot_general(
        coord_low, w_coord, (((0,), (0,)), ((), ())), preferred_element_type=jnp.float32
    )
    upstream = (
        upstream + logit_low.astype(jnp.float32)[:, None] * w_beta.astype(jnp.float32)[None, :]
    )
    count = w_layers.shape[0]
    weight_grads = [None] * count
    bias_grads = [None] * count
    for layer_num in range(count - 1, -1, -1):
        pre = preacts[layer_num]
        sig = jax.nn.sigmoid(pre)
        local = (upstream * sig * (1.0 + pre * (1.0 - sig))).astype(jnp.bfloat16)
        weight_grad = lax.dot_general(
            states[layer_num], local, (((0,), (0,)), ((), ())), preferred_element_type=jnp.float32
        )
        bias_grad = jnp.sum(local.astype(jnp.float32), 0)
        if layer_num > 0:
            upstream = lax.dot_general(
                local,
                w_layers[layer_num],
                (((1,), (1,)), ((), ())),
                preferred_element_type=jnp.float32,
            )
        weight_grads[layer_num] = weight_grad
        bias_grads[layer_num] = bias_grad
    grad_w_layers = jnp.stack(weight_grads)
    grad_b_layers = jnp.stack(bias_grads)
    grad_w_layers, grad_b_layers, grad_coord_w, grad_beta_w, loss_local = lax.psum(
        (grad_w_layers, grad_b_layers, grad_coord_w, grad_beta_w, loss_local), ("layer", "phi")
    )
    return (grad_w_layers, grad_b_layers, grad_coord_w, grad_beta_w, loss_local)


def solution(mesh):
    return jax.shard_map(
        on_device,
        mesh=mesh,
        in_specs=(
            P(("layer", "phi"), None),
            P(),
            P(),
            P(),
            P(),
            P(("layer", "phi")),
            P(("layer", "phi")),
            P(("layer", "phi")),
        ),
        out_specs=(P(), P(), P(), P(), P()),
        check_vma=False,
    )
```

profile of v0, /device:TPU:2, one launch (start us, length us, event | category | flops | bytes accessed | tf_op | source)
XLA Modules:
  0.0 1170.9 jit_solution(12711560222220822224)
XLA Ops:
  7.3 0.7 reshape.37
  8.0 0.7 broadcast_subtract_fusion
  8.7 0.8 fusion.82
  9.5 1.1 convolution_add_fusion.4
  11.5 0.7 copy-done.3
  12.2 0.6 multiply_reduce_fusion.3
  13.0 0.6 copy-done.7
  14.1 626.3 %all_gather.3 = f32[17,2048]{0,1:T(8,128)S(1)} all-gather(f32[17,8]{0,1:T(8,128)S(1)} %pad_maximum_fusion.1), channel_id=1, replica_groups=mesh['layer'=16,'phi'=16] {'layer','phi'}, dimensions={1}, use_global_device_ids=true | all-gather | bytes 139808 | tf_op jit(solution)/shard_map/all_gather | solution.py:109
  640.8 0.7 copy-done.5
  641.5 11.6 while.22
  641.6 1.3 multiply_reduce_fusion.8
  642.9 0.5 fusion.131
  643.7 0.6 fusion.132
  644.5 1.3 multiply_reduce_fusion.8
  645.8 0.5 fusion.131
  646.7 0.6 fusion.132
  647.4 1.3 multiply_reduce_fusion.8
  648.7 0.5 fusion.131
  649.6 0.6 fusion.132
  650.3 1.3 multiply_reduce_fusion.8
  652.5 0.6 fusion.132
  653.1 0.7 copy-done.1
  653.9 0.6 copy-done.6
  654.5 0.8 fusion.25
  656.7 243.4 %all-reduce.7.cloned.1.call-done = f32[17,2048]{1,0:T(8,128)} async-done(((f32[17,2048]{1,0:T(8,128)}), f32[17,2048]{1,0:T(8,128)}) %all-reduce.7.cloned.1.call-update) | async-done | bytes 139280
  900.1 0.9 fusion.41
  901.0 0.6 fusion.81
  901.6 0.9 fusion.23
  905.2 1.0 pad_maximum_fusion
  906.6 75.0 %all-reduce.1 = (f32[4,256]{1,0:T(4,128)}, f32[16,256]{1,0:T(8,128)}, f32[256]{0:T(256)}, f32[]{:T(128)}) all-reduce(f32[4,256]{1,0:T(4,128)S(1)} %pad_maximum_fusion.2, f32[16,256]{1,0:T(8,128)S(1)} %fusion.85, f32[256]{0:T(256)S(1)} %bitcast.138, f32[]{:T(128)S(6)} %add.271), channel_id=1, replica_groups=mesh['layer'=16,'phi'=16] {'layer','phi'}, use_global_device_ids=true, to_apply=%region_14.15 | all-reduce | flops 5377 | bytes 43016 | tf_op jit(solution)/shard_map/psum | solution.py:179
  981.6 180.0 %all-reduce.5.cloned.1.call-done = f32[4,256,256]{1,2,0:T(8,128)} async-done(((f32[4,256,256]{1,2,0:T(8,128)}), f32[4,256,256]{1,2,0:T(8,128)}) %all-reduce.5.cloned.1.call-update) | async-done | bytes 1048592 | tf_op jit(solution)/shard_map/psum | solution.py:179
  1161.6 2.5 copy.30
  (79 shorter events, 6.5 us)
Async XLA Ops:
  7.2 2.4 copy-start
  7.2 3.4 copy-start.2
  7.2 892.9 %all-reduce.7.cloned.1.call-start = ((), (), s32[]{:S(2)}) async-start(), calls=%async_computation.1 | async-start | bytes 393216
  11.3 1.5 copy-start.4
  11.5 0.7 copy-start.3
  13.0 0.7 copy-start.7
  640.8 0.7 copy-start.5
  653.1 0.7 copy-start.1
  653.8 507.8 %all-reduce.5.cloned.1.call-start = ((), (), s32[]{:S(2)}) async-start(), calls=%async_computation | async-start | bytes 2097152 | tf_op jit(solution)/shard_map/psum | solution.py:179
  653.9 0.7 copy-start.6
Sparse Core Ops, SparseCore 0:
  653.9 246.1 all-reduce.6
  906.4 255.1 all-reduce.4
where the time goes:
time: 1170 us
  blocking collectives  701 us (60%)
  waiting for transfers between devices  423 us (36%)
  matrix products  18.3 us (2%)
  between operations  16.2 us (1%)
    all_gather x1, blocking collectives, on_device(): piece = lax.all_gather(own_rows, ('layer', 'phi'), axis=1, tiled=True)  626 us
    unnamed x3, waiting for transfers between devices  243 us
    psum x1, waiting for transfers between devices, on_device(): lax.psum((grad_w_layers, grad_b_layers, grad_coord_w, grad_beta_w, loss_l...  180 us
    psum x1, blocking collectives, on_device(): lax.psum((grad_w_layers, grad_b_layers, grad_coord_w, grad_beta_w, loss_l...  75 us
  transfers between devices with their start and end apart: 2, of which 2 were waited for; matrix products, arithmetic and copies ran while one was open for 0% of the time, Pallas kernels for 0%

commit v1 on v0

--- a/solution.py
+++ b/solution.py
@@ -106,7 +106,15 @@
         jnp.zeros(coords.shape, jnp.float32),
         jnp.zeros((own_rows.shape[0], total_points), jnp.float32),
     )
-    piece = lax.all_gather(own_rows, ("layer", "phi"), axis=1, tiled=True)
+    blocks_here = []
+    for _ in range(lax.axis_size(("layer", "phi"))):
+        blocks_here.append(own_rows)
+    piece = jnp.concatenate(
+        lax.all_to_all(
+            jnp.stack(blocks_here, axis=0), ("layer", "phi"), concat_axis=0, split_axis=0
+        ),
+        1,
+    )
     width = piece.shape[1]
 
     def one_block(state, offset, cols):

time: 1170 us -> 574 us (0.49)
  blocking collectives: 701 us -> 74.9 us
  starting transfers between devices: 0.08 us -> 14.8 us
    all_gather x1 -> x0, blocking collectives: 626 us -> none  [on_device(): piece = lax.all_gather(own_rows, ('layer', 'phi'), axis=1, tiled=True)]
    all_to_all x0 -> x1, starting transfers between devices: none -> 14.7 us  [on_device(): lax.all_to_all(jnp.stack(blocks_here, axis=0), ('layer', 'phi'), concat_a...]
    all_to_all x0 -> x1, waiting for transfers between devices: none -> 11.9 us  [on_device(): lax.all_to_all(jnp.stack(blocks_here, axis=0), ('layer', 'phi'), concat_a...]
  transfers between devices with their start and end apart: 2 -> 3, of which waited for: 2 -> 3; matrix products, arithmetic and copies ran while one was open for 0% -> 0% of each run, Pallas kernels for 0% -> 0%
where the time goes in v1:
time: 574 us; the launch traced here: 573 us
  waiting for transfers between devices  433 us (75%)
  blocking collectives  74.9 us (13%)
  matrix products  18.8 us (3%)
  between operations  16.2 us (3%)
  starting transfers between devices  14.8 us (3%)
  local copies, waits for them, and re-layouts  11.4 us (2%)
    unnamed x3, waiting for transfers between devices  241 us
    psum x1, waiting for transfers between devices, on_device(): lax.psum((grad_w_layers, grad_b_layers, grad_coord_w, grad_beta_w, loss_l...  180 us
    psum x1, blocking collectives, on_device(): lax.psum((grad_w_layers, grad_b_layers, grad_coord_w, grad_beta_w, loss_l...  74.9 us
    all_to_all x1, starting transfers between devices, on_device(): lax.all_to_all(jnp.stack(blocks_here, axis=0), ('layer', 'phi'), concat_a...  14.7 us
    all_to_all x1, waiting for transfers between devices, on_device(): lax.all_to_all(jnp.stack(blocks_here, axis=0), ('layer', 'phi'), concat_a...  11.9 us
  transfers between devices with their start and end apart: 3, of which 3 were waited for; matrix products, arithmetic and copies ran while one was open for 0% of the time, Pallas kernels for 0%

profile of v1, /device:TPU:2, one launch (start us, length us, event | category | flops | bytes accessed | tf_op | source)
XLA Modules:
  0.0 573.3 jit_solution(9517267390154085301)
XLA Ops:
  7.2 0.8 fusion.82
  8.1 1.1 convolution_add_fusion.4
  10.1 0.9 multiply_convert_fusion
  11.9 0.7 copy-done.3
  12.6 0.6 multiply_reduce_fusion.3
  13.2 0.7 copy-done.7
  14.4 1.5 reshape.59
  16.0 14.7 %all-to-all-start = ((f32[256,1,136]{2,1,0:T(1,128)}), f32[256,1,136]{2,1,0:T(1,128)S(1)}, u32[]{:S(2)}, u32[]{:S(2)}) async-start(f32[256,1,136]{2,1,0:T(1,128)} %reshape.59), calls=%async_computation | async-start | bytes 524288 | tf_op jit(solution)/shard_map/all_to_all | solution.py:113
  30.7 0.8 fusion.25
  32.8 11.9 %all-to-all-done = f32[256,1,136]{2,1,0:T(1,128)S(1)} async-done(((f32[256,1,136]{2,1,0:T(1,128)}), f32[256,1,136]{2,1,0:T(1,128)S(1)}, u32[]{:S(2)}, u32[]{:S(2)}) %all-to-all-start) | async-done | bytes 139296 | tf_op jit(solution)/shard_map/all_to_all | solution.py:113
  45.3 1.3 reduce
  47.4 0.7 copy-done.5
  48.0 11.6 %while.22 = (s32[]{:T(128)}, f32[256]{0:T(256)S(1)}, f32[256]{0:T(256)S(1)}, f32[16,256]{1,0:T(8,128)S(1)}, f32[17,2048]{1,0:T(8,128)S(1)}, /*index=5*/f32[256]{...) while((s32[]{:T(128)}, f32[256]{0:T(256)S(1)}, ...), condition=%wide.region_6.7_spmd.clone, body=%wide.region_1.6_spmd.clone.sunk | while | flops 80528904 | bytes 2975734 | solution.py:131
  48.1 1.3 multiply_reduce_fusion.8
  50.0 0.6 fusion.131
  51.0 1.3 multiply_reduce_fusion.8
  52.9 0.6 fusion.131
  53.9 1.3 multiply_reduce_fusion.8
  55.8 0.6 fusion.131
  56.8 1.3 multiply_reduce_fusion.8
  58.7 0.6 fusion.131
  59.7 0.6 copy-done.1
  60.5 240.6 %all-reduce.7.cloned.1.call-done = f32[17,2048]{1,0:T(8,128)} async-done(((f32[17,2048]{1,0:T(8,128)}), f32[17,2048]{1,0:T(8,128)}) %all-reduce.7.cloned.1.call-update) | async-done | bytes 139280
  301.1 0.9 fusion.41
  302.0 0.6 fusion.81
  302.6 0.9 fusion.23
  303.8 0.7 copy-done.9
  304.7 0.7 copy-done.11
  307.6 1.0 pad_maximum_fusion
  309.0 74.9 %all-reduce.1 = (f32[4,256]{1,0:T(4,128)}, f32[16,256]{1,0:T(8,128)}, f32[256]{0:T(256)}, f32[]{:T(128)}) all-reduce(f32[4,256]{1,0:T(4,128)S(1)} %pad_maximum_fusion.2, f32[16,256]{1,0:T(8,128)S(1)} %fusion.85, f32[256]{0:T(256)S(1)} %bitcast.146, f32[]{:T(128)S(6)} %add.271), channel_id=1, replica_groups=mesh['layer'=16,'phi'=16] {'layer','phi'}, use_global_device_ids=true, to_apply=%region_14.15 | all-reduce | flops 5377 | bytes 43016 | tf_op jit(solution)/shard_map/psum | solution.py:187
  383.9 180.1 %all-reduce.5.cloned.1.call-done = f32[4,256,256]{1,2,0:T(8,128)} async-done(((f32[4,256,256]{1,2,0:T(8,128)}), f32[4,256,256]{1,2,0:T(8,128)}) %all-reduce.5.cloned.1.call-update) | async-done | bytes 1048592 | tf_op jit(solution)/shard_map/psum | solution.py:187
  563.9 2.5 copy.36
  (96 shorter events, 10.0 us)
Async XLA Ops:
  7.2 0.9 copy-start
  7.2 0.9 copy-start.6
  7.2 2.0 copy-start.2
  9.4 0.7 copy-start.10
  10.1 0.9 copy-start.8
  11.0 0.7 copy-start.4
  11.9 0.7 copy-start.3
  13.2 0.7 copy-start.7
  16.0 28.8 %all-to-all-start = ((f32[256,1,136]{2,1,0:T(1,128)}), f32[256,1,136]{2,1,0:T(1,128)S(1)}, u32[]{:S(2)}, u32[]{:S(2)}) async-start(f32[256,1,136]{2,1,0:T(1,128)} %reshape.59), calls=%async_computation | async-start | bytes 524288 | tf_op jit(solution)/shard_map/all_to_all | solution.py:113
  30.6 270.5 %all-reduce.7.cloned.1.call-start = ((), (), s32[]{:S(2)}) async-start(), calls=%async_computation.2 | async-start | bytes 393216
  47.3 0.7 copy-start.5
  59.6 0.7 copy-start.1
  59.6 243.9 %copy-start.12 = (f32[256,256]{1,0:T(8,128)S(1)}, f32[256,256]{1,0:T(8,128)}, u32[]{:S(2)}) copy-start(f32[256,256]{1,0:T(8,128)} %get-tuple-element.386) | copy-start | bytes 786436
  60.3 503.6 %all-reduce.5.cloned.1.call-start = ((), (), s32[]{:S(2)}) async-start(), calls=%async_computation.1 | async-start | bytes 2097152 | tf_op jit(solution)/shard_map/psum | solution.py:187
  303.5 1.0 copy-start.9
  304.5 0.9 copy-start.11
Sparse Core Ops, SparseCore 0:
  60.4 240.6 all-reduce.6
  308.8 255.1 all-reduce.4
